TPU v7x, 512 devices: a whole 4x8x8 slice. The times are simulated.
512 devices in a mesh: seq: 64 (over x, z, core), head: 8 (over y).
Axes of the slice: x: 4, y: 8, z: 8, core: 2. Of those that a mesh axis runs over, the one named last changes fastest.
Arguments:
- queries: bfloat16 [16384, 4096], P('seq', 'head'), may hold values from -6 to 6
- keys: bfloat16 [16384, 4096], P('seq', 'head'), may hold values from -6 to 6
- values: bfloat16 [16384, 4096], P('seq', 'head'), may hold values from -6 to 6
- gate: bfloat16 [16384, 4096], P('seq', 'head'), may hold values from -6 to 6
- residual: bfloat16 [16384, 4096], P('seq', 'head'), may hold values from -40 to 40
- log_decay: float32 [16384, 32], P('seq', 'head'), may hold values from -1 to 0, as said below
- out_weight: bfloat16 [4096, 4096], P('seq', 'head'), may hold values from -0.09375 to 0.09375
- norm_gain: bfloat16 [4096], P('head'), may hold values from 0.099609375 to 1.8984375
- kv_weight: bfloat16 [4096, 2048], P('seq', 'head'), may hold values from -0.09375 to 0.09375
Outputs:
- cache_keys: bfloat16 [16384, 1024], P('seq', 'head')
- cache_values: bfloat16 [16384, 1024], P('seq', 'head')
Inputs may be any that keep to these rules, and one draw needn't show every extreme that they name: `log_decay`: every entry is negative.
All inputs are finite; a program needn't handle non-finite values.
Results may differ from a plain program's by a relative error of at most 0.015.
Values may be sent and summed in bfloat16 or wider, within the bound.
A program may use at most 64 MiB of HBM per device.

v0:
```python
import jax
import jax.numpy as jnp
from jax import lax
from jax.sharding import PartitionSpec as P

HIGHEST = lax.Precision.HIGHEST


def entering(part, axis, combine, identity):
    place = lax.axis_index(axis)
    gathered = jax.tree.map(lambda a: lax.all_gather(a, axis), part)
    state = jax.tree.map(lambda a, e: jnp.zeros_like(a) + jnp.asarray(e, a.dtype), part, identity)

    def one(step, state):
        return combine(
            state, jax.tree.map(lambda a: lax.dynamic_index_in_dim(a, step, 0, False), gathered)
        )

    return lax.fori_loop(0, place, one, state)


def local_retention(queries, keys, values, log_decay, block):
    tokens, heads, width = queries.shape
    count = tokens // block

    def to_blocks(array):
        return array.reshape((count, block) + array.shape[1:])

    lower = jnp.arange(block)[:, None] >= jnp.arange(block)[None, :]

    def advance(carry, inputs):
        state, offset = carry
        query_block, key_block, value_block, decay_block = inputs
        within = jnp.cumsum(decay_block, axis=0)
        spread = within[:, None, :] - within[None, :, :]
        factor = jnp.where(
            lower[:, :, None], jnp.exp(jnp.where(lower[:, :, None], spread, 0.0)), 0.0
        )
        scores = jnp.einsum(
            "ihd,jhd->hij", query_block, key_block, preferred_element_type=jnp.float32
        )
        weighted = scores * jnp.transpose(factor, (2, 0, 1))
        values_wide = value_block.astype(jnp.float32)
        intra = jnp.einsum("hij,jhd->ihd", weighted, values_wide, precision=HIGHEST)
        query_wide = query_block.astype(jnp.float32)
        carried = jnp.exp(within)[:, :, None] * jnp.einsum(
            "ihd,hde->ihe", query_wide, state, precision=HIGHEST
        )
        ending = within[-1]
        key_wide = key_block.astype(jnp.float32) * jnp.exp(ending[None, :] - within)[:, :, None]
        fresh = jnp.exp(ending)[:, None, None] * state + jnp.einsum(
            "jhd,jhe->hde", key_wide, values_wide, precision=HIGHEST
        )
        return ((fresh, offset + ending), (intra + carried, offset[None, :] + within))

    start = (jnp.zeros((heads, width, width), jnp.float32), jnp.zeros((heads,), jnp.float32))
    final, stacked = lax.scan(
        advance,
        start,
        (to_blocks(queries), to_blocks(keys), to_blocks(values), to_blocks(log_decay)),
    )
    return (
        stacked[0].reshape(tokens, heads, width),
        stacked[1].reshape(tokens, heads),
        final[0],
        final[1],
    )


def combine_states(earlier, later):
    return (earlier[0] * later[0], later[0][:, None, None] * earlier[1] + later[1])


def on_device(queries, keys, values, gate, residual, log_decay, out_weight, norm_gain, kv_weight):
    tokens = queries.shape[0]
    heads = log_decay.shape[1]
    width = queries.shape[1] // heads
    shaped = [array.reshape(tokens, heads, width) for array in (queries, keys, values)]
    partial_out, running, state, offset = local_retention(
        shaped[0], shaped[1], shaped[2], log_decay, min(512, tokens)
    )
    identity = (jnp.ones((heads,), jnp.float32), jnp.zeros((heads, width, width), jnp.float32))
    scan_decay, incoming = entering((jnp.exp(offset), state), "seq", combine_states, identity)
    retained = partial_out + jnp.exp(running)[:, :, None] * jnp.einsum(
        "thd,hde->the", shaped[0].astype(jnp.float32), incoming, precision=HIGHEST
    )
    scale = lax.rsqrt(jnp.mean(retained * retained, axis=2, keepdims=True) + 1e-06)
    mixed = (
        jax.nn.silu(gate.astype(jnp.float32)) * (retained * scale).reshape(tokens, heads * width)
    ).astype(jnp.bfloat16)
    all_heads = lax.all_gather(mixed, "head", axis=1, tiled=True)
    out_full, kv_full = (
        lax.all_gather(out_weight, "seq", axis=0, tiled=True),
        lax.all_gather(kv_weight, "seq", axis=0, tiled=True),
    )
    branch = jnp.dot(all_heads, out_full, preferred_element_type=jnp.float32)
    hidden = (residual.astype(jnp.float32) + branch).astype(jnp.bfloat16)
    wide = hidden.astype(jnp.float32)
    squares = lax.psum(jnp.sum(wide * wide, axis=1), "head")
    features = wide.shape[1] * lax.axis_size("head")
    inverse = lax.rsqrt(squares[:, None] / features + 1e-06)
    local_norm = (wide * inverse * norm_gain.astype(jnp.float32)[None, :]).astype(jnp.bfloat16)
    normalized = lax.all_gather(local_norm, "head", axis=1, tiled=True)
    projected = jnp.dot(normalized, kv_full, preferred_element_type=jnp.float32)
    cache_heads = kv_weight.shape[1] // (2 * width)
    arranged = projected.reshape(tokens, cache_heads, 2, width)
    cache_keys = arranged[:, :, 0, :].reshape(tokens, cache_heads * width).astype(jnp.bfloat16)
    cache_values = arranged[:, :, 1, :].reshape(tokens, cache_heads * width).astype(jnp.bfloat16)
    return (cache_keys, cache_values)


def solution(mesh):
    placed = (
        P("seq", "head"),
        P("seq", "head"),
        P("seq", "head"),
        P("seq", "head"),
        P("seq", "head"),
        P("seq", "head"),
        P("seq", "head"),
        P("head"),
        P("seq", "head"),
    )
    return jax.shard_map(
        on_device,
        mesh=mesh,
        in_specs=placed,
        out_specs=(P("seq", "head"), P("seq", "head")),
        check_vma=False,
    )
```

profile of v0, /device:TPU:2, one launch (start us, length us, event | category | flops | bytes accessed | tf_op | source)
XLA Modules:
  0.0 390.9 jit_solution(8764286394529594663)
XLA Ops:
  8.0 1.2 reduce-window.6
  9.8 1.1 copy.73
  10.9 2.0 convolution_add_fusion.1
  13.8 44.7 %all-gather.1 = f32[64,1,4]{2,1,0:T(1,128)S(1)} all-gather(f32[1,1,4]{2,1,0:T(1,128)S(1)} %bitcast.97), channel_id=1, replica_groups=mesh['seq'=64,'head'=8] {'seq'}, dimensions={0}, use_global_device_ids=true | all-gather | bytes 1040 | tf_op jit(solution)/shard_map/all_gather | solution.py:11
  59.4 63.1 %all-gather.16.cloned.1.call-done = f32[256,128,128]{2,1,0:T(8,128)} async-done(((f32[4,128,128]{2,1,0:T(8,128)}), f32[256,128,128]{2,1,0:T(8,128)}) %all-gather.16.cloned.1.call-update) | async-done | bytes 16777232 | tf_op jit(solution)/shard_map/all_gather | solution.py:11
  122.5 17.8 %while.3 = (s32[]{:T(128)}, f32[4,128,128]{2,1,0:T(8,128)S(1)}, s32[]{:T(128)}, f32[64,4]{1,0:T(8,128)S(1)}, f32[64,4,128,128]{3,2,1,0:T(8,128)}, /*index=5*/s32[]{:T(128)}, s32[]{:T(128)}, s32[]{:T(128)}) while((s32[]{:T(128)}, f32[4,128,128]{2,1,0:T(8,128)S(1)}, s32[]{:T(128)}, f32[64,4]{1,0:T(8,128)S(1)}, f32[64,4,128,128]{3,2,1,0:T(8,128)}, ...), condition=%wide.region_3.4_spmd, body=%wide.region_2.3_spmd.sunk | while | flops 131077 | bytes 786607 | solution.py:19
  122.6 1.1 bitcast_add_fusion.2
  123.7 1.1 bitcast_add_fusion.2
  124.8 1.1 bitcast_add_fusion.2
  125.9 1.1 bitcast_add_fusion.2
  127.0 1.1 bitcast_add_fusion.2
  128.1 1.1 bitcast_add_fusion.2
  129.2 1.1 bitcast_add_fusion.2
  130.4 1.1 bitcast_add_fusion.2
  137.0 1.1 bitcast_add_fusion.2
  138.1 1.1 bitcast_add_fusion.2
  139.2 1.1 bitcast_add_fusion.2
  143.4 64.4 %all-gather.10.cloned.1.call-done = bf16[4096,512]{1,0:T(8,128)(2,1)} async-done(((bf16[64,512]{1,0:T(8,128)(2,1)}), bf16[4096,512]{1,0:T(8,128)(2,1)}) %all-gather.10.cloned.1.call-update) | async-done | bytes 4194320 | tf_op jit(solution)/shard_map/all_gather | solution.py:93
  207.8 43.4 %all-gather.8.cloned.1.call-done = bf16[256,4096]{1,0:T(8,128)(2,1)} async-done(((bf16[256,512]{1,0:T(8,128)(2,1)}), bf16[256,4096]{1,0:T(8,128)(2,1)}) %all-gather.8.cloned.1.call-update) | async-done | bytes 2097168 | tf_op jit(solution)/shard_map/all_gather | solution.py:91
  251.2 4.2 %multiply_reduce_fusion = (f32[256]{0:T(256)S(1)}, f32[256,512]{1,0:T(8,128)S(1)}) fusion(bf16[256,4096]{1,0:T(8,128)(2,1)} %all-gather.8.cloned.1.call-done, bf16[4096,512]{1,0:T(8,128)(2,1)} %all-gather.10.cloned.1.call-done, bf16[256,512]{1,0:T(8,128)(2,1)S(1)} %copy-done.4), kind=kOutput, calls=%fused_computation.22 | convolution fusion | flops 1074528000 | bytes 7078912 | tf_op jit(solution)/shard_map/dot_general | solution.py:96
  255.3 16.2 %psum.7 = f32[256]{0:T(256)S(1)} all-reduce(f32[256]{0:T(256)S(1)} %get-tuple-element.97), channel_id=1, replica_groups=mesh['seq'=64,'head'=8] {'head'}, use_global_device_ids=true, to_apply=%region_6.7 | all-reduce | flops 256 | bytes 2048 | tf_op jit(solution)/shard_map/psum | solution.py:99
  272.4 63.8 %all-gather.14.cloned.1.call-done = bf16[4096,256]{1,0:T(8,128)(2,1)} async-done(((bf16[64,256]{1,0:T(8,128)(2,1)}), bf16[4096,256]{1,0:T(8,128)(2,1)}) %all-gather.14.cloned.1.call-update) | async-done | bytes 2097168 | tf_op jit(solution)/shard_map/all_gather | solution.py:94
  336.2 43.6 %all-gather.12.cloned.1.call-done = bf16[256,4096]{1,0:T(8,128)(2,1)} async-done(((bf16[256,512]{1,0:T(8,128)(2,1)}), bf16[256,4096]{1,0:T(8,128)(2,1)}) %all-gather.12.cloned.1.call-update) | async-done | bytes 2097168 | tf_op jit(solution)/shard_map/all_gather | solution.py:103
  379.8 3.1 convolution_convert_fusion
  (68 shorter events, 13.8 us)
Async XLA Ops:
  7.2 51.4 %copy-start = (bf16[256,512]{1,0:T(8,128)(2,1)S(1)}, bf16[256,512]{1,0:T(8,128)(2,1)}, u32[]{:S(2)}) copy-start(bf16[256,512]{1,0:T(8,128)(2,1)} %param.11) | copy-start | bytes 786436
  7.2 115.3 %all-gather.16.cloned.1.call-start = ((), (), s32[]{:S(2)}) async-start(), calls=%async_computation.4 | async-start | bytes 17039360 | tf_op jit(solution)/shard_map/all_gather | solution.py:11
  13.0 194.8 %all-gather.10.cloned.1.call-start = ((), (), s32[]{:S(2)}) async-start(), calls=%async_computation.1 | async-start | bytes 4259840 | tf_op jit(solution)/shard_map/all_gather | solution.py:93
  13.8 237.4 %all-gather.8.cloned.1.call-start = ((), (), s32[]{:S(2)}) async-start(), calls=%async_computation | async-start | bytes 2359296 | tf_op jit(solution)/shard_map/all_gather | solution.py:91
  122.5 18.2 %copy-start.1 = (bf16[256,512]{1,0:T(8,128)(2,1)S(1)}, bf16[256,512]{1,0:T(8,128)(2,1)}, u32[]{:S(2)}) copy-start(bf16[256,512]{1,0:T(8,128)(2,1)} %param.13) | copy-start | bytes 786436
  140.8 1.1 copy-start.2
  141.5 1.8 copy-start.3
  141.5 109.7 %copy-start.4 = (bf16[256,512]{1,0:T(8,128)(2,1)S(1)}, bf16[256,512]{1,0:T(8,128)(2,1)}, u32[]{:S(2)}) copy-start(bf16[256,512]{1,0:T(8,128)(2,1)} %param.15) | copy-start | bytes 786436
  142.7 193.4 %all-gather.14.cloned.1.call-start = ((), (), s32[]{:S(2)}) async-start(), calls=%async_computation.3 | async-start | bytes 2129920 | tf_op jit(solution)/shard_map/all_gather | solution.py:94
  143.3 236.5 %all-gather.12.cloned.1.call-start = ((), (), s32[]{:S(2)}) async-start(), calls=%async_computation.2 | async-start | bytes 2359296 | tf_op jit(solution)/shard_map/all_gather | solution.py:103
Sparse Core Ops, SparseCore 0:
  13.1 109.3 all-gather.15
  125.8 81.8 all-gather.9
  209.9 41.2 all-gather.7
  254.4 81.7 all-gather.13
  338.1 41.6 all-gather.11
where the time goes:
time: 393 us; the launch traced here: 391 us
  waiting for transfers between devices  280 us (71%)
  blocking collectives  60.9 us (15%)
  other arithmetic  20.2 us (5%)
  between operations  14 us (4%)
  matrix products  11.3 us (3%)
  local copies, waits for them, and re-layouts  4.19 us (1%)
    all_gather x1, waiting for transfers between devices, on_device(): lax.all_gather(out_weight, 'seq', axis=0, tiled=True)  64.4 us
    all_gather x1, waiting for transfers between devices, on_device(): lax.all_gather(kv_weight, 'seq', axis=0, tiled=True)  63.8 us
    all_gather x1, waiting for transfers between devices, entering(): gathered = jax.tree.map(lambda a: lax.all_gather(a, axis), part)  63.1 us
    all_gather x1, blocking collectives, entering(): gathered = jax.tree.map(lambda a: lax.all_gather(a, axis), part)  44.7 us
    all_gather x1, waiting for transfers between devices, on_device(): normalized = lax.all_gather(local_norm, 'head', axis=1, tiled=True)  43.6 us
    all_gather x1, waiting for transfers between devices, on_device(): all_heads = lax.all_gather(mixed, 'head', axis=1, tiled=True)  43.4 us
    add x16, other arithmetic, combine_states(): later[0][:, None, None] * earlier[1] + later[1]  17 us
    psum x1, blocking collectives, on_device(): squares = lax.psum(jnp.sum(wide * wide, axis=1), 'head')  16.2 us
  transfers between devices with their start and end apart: 5, of which 5 were waited for; matrix products, arithmetic and copies ran while one was open for 6% of the time, Pallas kernels for 0%

commit v1 on v0

--- a/solution.py
+++ b/solution.py
@@ -4,6 +4,16 @@
 from jax.sharding import PartitionSpec as P
 
 HIGHEST = lax.Precision.HIGHEST
+
+
+def pack_sectors_on_mesh(my_data):
+    ax_name = "seq"
+    n_chips = lax.psum(1, ax_name)
+    arrivals = [n_chips if m == 0 else 1 for m in range(my_data.ndim)]
+    r1 = lax.all_to_all(
+        jnp.tile(my_data, arrivals), ax_name, split_axis=0, concat_axis=0, tiled=True
+    )
+    return r1
 
 
 def entering(part, axis, combine, identity):
@@ -91,7 +101,7 @@
     all_heads = lax.all_gather(mixed, "head", axis=1, tiled=True)
     out_full, kv_full = (
         lax.all_gather(out_weight, "seq", axis=0, tiled=True),
-        lax.all_gather(kv_weight, "seq", axis=0, tiled=True),
+        pack_sectors_on_mesh(kv_weight),
     )
     branch = jnp.dot(all_heads, out_full, preferred_element_type=jnp.float32)
     hidden = (residual.astype(jnp.float32) + branch).astype(jnp.bfloat16)

time: 393 us -> 329 us (0.84)
  waiting for transfers between devices: 280 us -> 155 us
  starting transfers between devices: 0.2 us -> 57.5 us
    all_gather x1 -> x0, waiting for transfers between devices: 63.8 us -> none  [on_device(): lax.all_gather(kv_weight, 'seq', axis=0, tiled=True)]
    all_to_all x0 -> x1, starting transfers between devices: none -> 57.3 us  [pack_sectors_on_mesh(): lax.all_to_all(jnp.tile(my_data, arrivals), ax_name, split_axis=0, concat...]
    all_gather x1, waiting for transfers between devices: 64.4 us -> 7.22 us  [on_device(): lax.all_gather(out_weight, 'seq', axis=0, tiled=True)]
  transfers between devices with their start and end apart: 5 -> 5, of which waited for: 5 -> 4; matrix products, arithmetic and copies ran while one was open for 6% -> 9% of each run, Pallas kernels for 0% -> 0%
where the time goes in v1:
time: 329 us; the launch traced here: 327 us
  waiting for transfers between devices  155 us (47%)
  blocking collectives  60.7 us (18%)
  starting transfers between devices  57.5 us (17%)
  other arithmetic  20.2 us (6%)
  between operations  14 us (4%)
  matrix products  11.1 us (3%)
  local copies, waits for them, and re-layouts  7.91 us (2%)
    all_gather x1, waiting for transfers between devices, entering(): gathered = jax.tree.map(lambda a: lax.all_gather(a, axis), part)  63.1 us
    all_to_all x1, starting transfers between devices, pack_sectors_on_mesh(): lax.all_to_all(jnp.tile(my_data, arrivals), ax_name, split_axis=0, concat...  57.3 us
    all_gather x1, blocking collectives, entering(): gathered = jax.tree.map(lambda a: lax.all_gather(a, axis), part)  44.7 us
    all_gather x1, waiting for transfers between devices, on_device(): all_heads = lax.all_gather(mixed, 'head', axis=1, tiled=True)  43.8 us
    all_gather x1, waiting for transfers between devices, on_device(): normalized = lax.all_gather(local_norm, 'head', axis=1, tiled=True)  40 us
    add x16, other arithmetic, combine_states(): later[0][:, None, None] * earlier[1] + later[1]  17 us
    psum x1, blocking collectives, on_device(): squares = lax.psum(jnp.sum(wide * wide, axis=1), 'head')  16 us
    all_gather x1, waiting for transfers between devices, on_device(): lax.all_gather(out_weight, 'seq', axis=0, tiled=True)  7.22 us
  transfers between devices with their start and end apart: 5, of which 4 were waited for; matrix products, arithmetic and copies ran while one was open for 9% of the time, Pallas kernels for 0%

profile of v1, /device:TPU:2, one launch (start us, length us, event | category | flops | bytes accessed | tf_op | source)
XLA Modules:
  0.0 326.8 jit_solution(12163116581943568174)
XLA Ops:
  8.0 1.2 reduce-window.6
  9.8 1.1 copy.83
  10.9 2.0 convolution_add_fusion.1
  13.8 44.7 %all-gather.1 = f32[64,1,4]{2,1,0:T(1,128)S(1)} all-gather(f32[1,1,4]{2,1,0:T(1,128)S(1)} %bitcast.109), channel_id=1, replica_groups=mesh['seq'=64,'head'=8] {'seq'}, dimensions={0}, use_global_device_ids=true | all-gather | bytes 1040 | tf_op jit(solution)/shard_map/all_gather | solution.py:21
  59.4 63.1 %all-gather.13.cloned.1.call-done = f32[256,128,128]{2,1,0:T(8,128)} async-done(((f32[4,128,128]{2,1,0:T(8,128)}), f32[256,128,128]{2,1,0:T(8,128)}) %all-gather.13.cloned.1.call-update) | async-done | bytes 16777232 | tf_op jit(solution)/shard_map/all_gather | solution.py:21
  122.5 17.8 %while.3 = (s32[]{:T(128)}, f32[4,128,128]{2,1,0:T(8,128)S(1)}, s32[]{:T(128)}, f32[64,4]{1,0:T(8,128)S(1)}, f32[64,4,128,128]{3,2,1,0:T(8,128)}, /*index=5*/s32[]{:T(128)}, s32[]{:T(128)}, s32[]{:T(128)}) while((s32[]{:T(128)}, f32[4,128,128]{2,1,0:T(8,128)S(1)}, s32[]{:T(128)}, f32[64,4]{1,0:T(8,128)S(1)}, f32[64,4,128,128]{3,2,1,0:T(8,128)}, ...), condition=%wide.region_3.4_spmd, body=%wide.region_2.3_spmd.sunk | while | flops 131077 | bytes 786607 | solution.py:29
  122.6 1.1 bitcast_add_fusion.2
  123.7 1.1 bitcast_add_fusion.2
  124.8 1.1 bitcast_add_fusion.2
  125.9 1.1 bitcast_add_fusion.2
  127.0 1.1 bitcast_add_fusion.2
  128.1 1.1 bitcast_add_fusion.2
  129.2 1.1 bitcast_add_fusion.2
  138.1 1.1 bitcast_add_fusion.2
  139.2 1.1 bitcast_add_fusion.2
  142.7 1.6 tile.2
  144.3 57.3 %all-to-all-start = ((bf16[64,64,256]{2,1,0:T(8,128)(2,1)}), bf16[64,64,256]{2,1,0:T(8,128)(2,1)S(1)}, u32[]{:S(2)}, u32[]{:S(2)}) async-start(bf16[64,64,256]{2,1,0:T(8,128)(2,1)} %tile.2), calls=%async_computation | async-start | bytes 4194304 | tf_op jit(solution)/shard_map/all_to_all | solution.py:13
  201.7 7.2 %all-gather.9.cloned.1.call-done = bf16[4096,512]{1,0:T(8,128)(2,1)} async-done(((bf16[64,512]{1,0:T(8,128)(2,1)}), bf16[4096,512]{1,0:T(8,128)(2,1)}) %all-gather.9.cloned.1.call-update) | async-done | bytes 4194320 | tf_op jit(solution)/shard_map/all_gather | solution.py:103
  208.9 43.8 %all-gather.7.cloned.1.call-done = bf16[256,4096]{1,0:T(8,128)(2,1)} async-done(((bf16[256,512]{1,0:T(8,128)(2,1)}), bf16[256,4096]{1,0:T(8,128)(2,1)}) %all-gather.7.cloned.1.call-update) | async-done | bytes 2097168 | tf_op jit(solution)/shard_map/all_gather | solution.py:101
  252.7 4.1 %multiply_reduce_fusion = (f32[256]{0:T(256)S(1)}, f32[256,512]{1,0:T(8,128)S(1)}) fusion(bf16[256,4096]{1,0:T(8,128)(2,1)} %all-gather.7.cloned.1.call-done, bf16[4096,512]{1,0:T(8,128)(2,1)} %all-gather.9.cloned.1.call-done, bf16[256,512]{1,0:T(8,128)(2,1)S(1)} %copy-done.5), kind=kOutput, calls=%fused_computation.25 | convolution fusion | flops 1074528000 | bytes 7078912 | tf_op jit(solution)/shard_map/dot_general | solution.py:106
  256.8 16.0 %psum.7 = f32[256]{0:T(256)S(1)} all-reduce(f32[256]{0:T(256)S(1)} %get-tuple-element.97), channel_id=1, replica_groups=mesh['seq'=64,'head'=8] {'head'}, use_global_device_ids=true, to_apply=%region_6.7 | all-reduce | flops 256 | bytes 2048 | tf_op jit(solution)/shard_map/psum | solution.py:109
  273.7 2.9 copy.80
  276.6 40.0 %all-gather.11.cloned.1.call-done = bf16[256,4096]{1,0:T(8,128)(2,1)} async-done(((bf16[256,512]{1,0:T(8,128)(2,1)}), bf16[256,4096]{1,0:T(8,128)(2,1)}) %all-gather.11.cloned.1.call-update) | async-done | bytes 2097168 | tf_op jit(solution)/shard_map/all_gather | solution.py:113
  316.7 3.0 fusion.11
  (69 shorter events, 14.5 us)
Async XLA Ops:
  7.2 51.4 %copy-start = (bf16[256,512]{1,0:T(8,128)(2,1)S(1)}, bf16[256,512]{1,0:T(8,128)(2,1)}, u32[]{:S(2)}) copy-start(bf16[256,512]{1,0:T(8,128)(2,1)} %param.11) | copy-start | bytes 786436
  7.2 115.3 %all-gather.13.cloned.1.call-start = ((), (), s32[]{:S(2)}) async-start(), calls=%async_computation.4 | async-start | bytes 17039360 | tf_op jit(solution)/shard_map/all_gather | solution.py:21
  13.0 195.9 %all-gather.9.cloned.1.call-start = ((), (), s32[]{:S(2)}) async-start(), calls=%async_computation.2 | async-start | bytes 4259840 | tf_op jit(solution)/shard_map/all_gather | solution.py:103
  13.8 238.9 %all-gather.7.cloned.1.call-start = ((), (), s32[]{:S(2)}) async-start(), calls=%async_computation.1 | async-start | bytes 2359296 | tf_op jit(solution)/shard_map/all_gather | solution.py:101
  122.5 18.2 %copy-start.1 = (bf16[256,512]{1,0:T(8,128)(2,1)S(1)}, bf16[256,512]{1,0:T(8,128)(2,1)}, u32[]{:S(2)}) copy-start(bf16[256,512]{1,0:T(8,128)(2,1)} %param.13) | copy-start | bytes 786436
  140.7 1.1 copy-start.2
  141.5 1.2 copy-start.3
  144.3 57.4 %copy-start.4 = (bf16[512]{0:T(512)(128)(2,1)S(1)}, bf16[512]{0:T(512)(128)(2,1)}, u32[]{:S(2)}) copy-start(bf16[512]{0:T(512)(128)(2,1)} %param.18) | copy-start | bytes 3076
  144.3 108.4 %copy-start.5 = (bf16[256,512]{1,0:T(8,128)(2,1)S(1)}, bf16[256,512]{1,0:T(8,128)(2,1)}, u32[]{:S(2)}) copy-start(bf16[256,512]{1,0:T(8,128)(2,1)} %param.15) | copy-start | bytes 786436
  144.3 129.4 %all-to-all-start = ((bf16[64,64,256]{2,1,0:T(8,128)(2,1)}), bf16[64,64,256]{2,1,0:T(8,128)(2,1)S(1)}, u32[]{:S(2)}, u32[]{:S(2)}) async-start(bf16[64,64,256]{2,1,0:T(8,128)(2,1)} %tile.2), calls=%async_computation | async-start | bytes 4194304 | tf_op jit(solution)/shard_map/all_to_all | solution.py:13
  201.6 115.1 %all-gather.11.cloned.1.call-start = ((), (), s32[]{:S(2)}) async-start(), calls=%async_computation.3 | async-start | bytes 2359296 | tf_op jit(solution)/shard_map/all_gather | solution.py:113
Sparse Core Ops, SparseCore 0:
  13.1 109.3 all-gather.12
  125.8 82.9 all-gather.8
  211.0 41.6 all-gather.6
  273.8 42.8 all-gather.10
